TPU v7x, 32 devices: a whole 2x2x4 slice. The times are simulated.
32 devices in a mesh: dp: 8 (over z, y), tensor: 4 (over x, core).
Axes of the slice: x: 2, y: 2, z: 4, core: 2. Of those that a mesh axis runs over, the one named last changes fastest.
Arguments:
- tokens: bfloat16 [2, 128, 12288], P(None, 'dp', 'tensor'), may hold values from -6 to 6
- up_weight: bfloat16 [12288, 49152], P('tensor', 'dp'), may hold values from -0.0546875 to 0.0546875
- up_bias: bfloat16 [49152], P('dp'), may hold values from -3 to 3
- down_weight: bfloat16 [49152, 12288], P('dp', 'tensor'), may hold values from -0.02734375 to 0.02734375
- down_bias: bfloat16 [12288], P('tensor'), may hold values from -3 to 3
- active: int32 [2, 1, 384], P(None, None, 'dp'), may hold values from 0 to 1
Outputs:
- mixed: bfloat16 [2, 128, 12288], P(None, 'dp', 'tensor')
All inputs are finite; a program needn't handle non-finite values.
Results may differ from a plain program's by a relative error of at most 0.0042.
Values may be sent and summed in bfloat16 or wider, within the bound.
A program may use at most 128 MiB of HBM per device.

v0:
```python
import jax
import jax.numpy as jnp
from jax import lax
from jax.sharding import PartitionSpec as P

RBLK = 128


def activate(summed, up_bias, mask_table, first_row):
    row_count = summed.shape[0]
    blocks = mask_table.shape[1]
    row_ids = first_row + jnp.arange(row_count, dtype=jnp.int32)
    onehot = (
        row_ids[:, None] // RBLK == jnp.arange(mask_table.shape[0], dtype=jnp.int32)[None, :]
    ).astype(jnp.float32)
    row_mask = jnp.dot(onehot, mask_table.astype(jnp.float32))
    preact = jnp.maximum(summed + up_bias.astype(jnp.float32), 0.0)
    gated_rows = preact.reshape(row_count, blocks, -1) * row_mask[:, :, None]
    return gated_rows.reshape(row_count, -1).astype(jnp.bfloat16)


def local(tokens, up_weight, up_bias, down_weight, down_bias, active):
    results = []
    for step_index in range(tokens.shape[0]):
        local_rows = tokens[step_index]
        mask_table = active[step_index]
        partial_up = jnp.dot(
            lax.all_gather(local_rows, "dp", axis=0, tiled=True),
            up_weight,
            preferred_element_type=jnp.float32,
        )
        row_share = lax.psum_scatter(partial_up, "tensor", scatter_dimension=0, tiled=True)
        first_row = lax.axis_index("tensor") * row_share.shape[0]
        hidden_share = activate(row_share, up_bias, mask_table, first_row)
        hidden = lax.all_gather(hidden_share, "tensor", axis=0, tiled=True)
        mixed_rows = lax.psum_scatter(
            jnp.dot(hidden, down_weight, preferred_element_type=jnp.float32),
            "dp",
            scatter_dimension=0,
            tiled=True,
        )
        results.append((mixed_rows + down_bias.astype(jnp.float32)).astype(jnp.bfloat16))
    return jnp.stack(results)


def solution(mesh):
    placed = (
        P(None, "dp", "tensor"),
        P("tensor", "dp"),
        P("dp"),
        P("dp", "tensor"),
        P("tensor"),
        P(None, None, "dp"),
    )
    return jax.shard_map(
        local, mesh=mesh, in_specs=placed, out_specs=P(None, "dp", "tensor"), check_vma=False
    )
```

profile of v0, /device:TPU:0, one launch (start us, length us, event | category | flops | bytes accessed | tf_op | source)
XLA Modules:
  0.0 334.4 jit_solution(13566910101976938622)
XLA Ops:
  6.5 1.0 fusion.8
  7.5 33.9 %all-gather = bf16[1,128,3072]{2,1,0:T(8,128)(2,1)S(1)} all-gather(bf16[1,16,3072]{2,1,0:T(8,128)(2,1)S(1)} %get-tuple-element.5), channel_id=2, replica_groups=mesh['dp'=8,'tensor'=4] {'dp'}, dimensions={1}, use_global_device_ids=true | all-gather | bytes 884736 | tf_op jit(solution)/shard_map/all_gather | solution.py:28
  41.4 16.1 %fusion.4 = f32[128,6144]{1,0:T(8,128)} fusion(bf16[3072,6144]{1,0:T(8,128)(2,1)} %param.7, bf16[1,128,3072]{2,1,0:T(8,128)(2,1)S(1)} %all-gather), kind=kOutput, calls=%fused_computation.6 | convolution fusion | flops 4831838208 | bytes 41680896 | tf_op jit(solution)/shard_map/dot_general | solution.py:27
  57.5 0.0 reduce-scatter.9.cloned.1.call-start
  57.5 32.1 %all-gather.1 = bf16[1,128,3072]{2,1,0:T(8,128)(2,1)S(1)} all-gather(bf16[1,16,3072]{2,1,0:T(8,128)(2,1)S(1)} %get-tuple-element.6), channel_id=3, replica_groups=mesh['dp'=8,'tensor'=4] {'dp'}, dimensions={1}, use_global_device_ids=true | all-gather | bytes 884736 | tf_op jit(solution)/shard_map/all_gather | solution.py:28
  89.6 16.2 %fusion.2 = f32[128,6144]{1,0:T(8,128)} fusion(bf16[3072,6144]{1,0:T(8,128)(2,1)} %param.7, bf16[1,128,3072]{2,1,0:T(8,128)(2,1)S(1)} %all-gather.1), kind=kOutput, calls=%fused_computation.4 | convolution fusion | flops 4831838208 | bytes 41680896 | tf_op jit(solution)/shard_map/dot_general | solution.py:27
  105.9 0.0 all-gather.7.cloned.1.call-start
  106.0 0.6 copy-done
  106.6 0.1 broadcast_multiply_fusion.1
  106.7 38.1 %reduce-scatter.9.cloned.1.call-done = f32[32,6144]{1,0:T(8,128)} async-done(((f32[128,6144]{1,0:T(8,128)}), f32[32,6144]{1,0:T(8,128)}) %reduce-scatter.9.cloned.1.call-update) | async-done | bytes 786448 | tf_op jit(solution)/shard_map/reduce_scatter | solution.py:32
  144.8 0.3 mul.27
  145.1 0.3 mul.30
  145.3 3.0 fusion.1
  148.3 0.0 all-gather.5.cloned.1.call-start
  148.4 0.5 all-gather.5.cloned.1.call-update
  149.0 19.2 %all-gather.7.cloned.1.call-done = bf16[128,6144]{1,0:T(8,128)(2,1)} async-done(((bf16[32,6144]{1,0:T(8,128)(2,1)}), bf16[128,6144]{1,0:T(8,128)(2,1)}) %all-gather.7.cloned.1.call-update) | async-done | bytes 1572880 | tf_op jit(solution)/shard_map/all_gather | solution.py:35
  168.1 16.5 %fusion.10 = f32[128,3072]{1,0:T(8,128)} fusion(bf16[128,6144]{1,0:T(8,128)(2,1)} %all-gather.7.cloned.1.call-done, bf16[6144,3072]{1,0:T(8,128)(2,1)} %param.9), kind=kOutput, calls=%fused_computation.24 | convolution fusion | flops 4831838208 | bytes 40894464 | tf_op jit(solution)/shard_map/dot_general | solution.py:37
  184.7 0.2 reduce-scatter.7.cloned.1.call-start
  184.9 4.3 %all-gather.5.cloned.1.call-done = bf16[128,6144]{1,0:T(8,128)(2,1)} async-done(((bf16[32,6144]{1,0:T(8,128)(2,1)}), bf16[128,6144]{1,0:T(8,128)(2,1)}) %all-gather.5.cloned.1.call-update) | async-done | bytes 1572880 | tf_op jit(solution)/shard_map/all_gather | solution.py:35
  189.2 16.1 %fusion.9 = f32[128,3072]{1,0:T(8,128)} fusion(bf16[128,6144]{1,0:T(8,128)(2,1)} %all-gather.5.cloned.1.call-done, bf16[6144,3072]{1,0:T(8,128)(2,1)} %param.9), kind=kOutput, calls=%fused_computation.23 | convolution fusion | flops 4831838208 | bytes 40894464 | tf_op jit(solution)/shard_map/dot_general | solution.py:37
  205.3 52.9 %reduce-scatter.11.cloned.1.call-done = f32[16,3072]{1,0:T(8,128)} async-done(((f32[128,3072]{1,0:T(8,128)}), f32[16,3072]{1,0:T(8,128)}) %reduce-scatter.11.cloned.1.call-update) | async-done | bytes 196624 | tf_op jit(solution)/shard_map/reduce_scatter | solution.py:36
  258.2 67.6 %reduce-scatter.7.cloned.1.call-done = f32[16,3072]{1,0:T(8,128)} async-done(((f32[128,3072]{1,0:T(8,128)}), f32[16,3072]{1,0:T(8,128)}) %reduce-scatter.7.cloned.1.call-update) | async-done | bytes 196624 | tf_op jit(solution)/shard_map/reduce_scatter | solution.py:36
  325.8 1.0 fusion.6
  326.9 0.7 pad_maximum_fusion
  (17 shorter events, 0.2 us)
Async XLA Ops:
  6.5 100.2 %reduce-scatter.5.cloned.1.call-start = ((), (), s32[]{:S(2)}) async-start(), calls=%async_computation.4 | async-start | bytes 3932160 | tf_op jit(solution)/shard_map/reduce_scatter | solution.py:32
  57.5 87.3 %reduce-scatter.9.cloned.1.call-start = ((), (), s32[]{:S(2)}) async-start(), calls=%async_computation.7 | async-start | bytes 3932160 | tf_op jit(solution)/shard_map/reduce_scatter | solution.py:32
  105.9 0.7 copy-start
  105.9 0.7 copy-start.2
  105.9 62.2 %all-gather.7.cloned.1.call-start = ((), (), s32[]{:S(2)}) async-start(), calls=%async_computation.8 | async-start | bytes 1966080 | tf_op jit(solution)/shard_map/all_gather | solution.py:35
  148.3 40.9 %all-gather.5.cloned.1.call-start = ((), (), s32[]{:S(2)}) async-start(), calls=%async_computation.5 | async-start | bytes 1966080 | tf_op jit(solution)/shard_map/all_gather | solution.py:35
  148.9 109.3 %reduce-scatter.11.cloned.1.call-start = ((), (), s32[]{:S(2)}) async-start(), calls=%async_computation.9 | async-start | bytes 1769472 | tf_op jit(solution)/shard_map/reduce_scatter | solution.py:36
  184.7 20.6 %copy-start.1 = (bf16[3072]{0:T(1024)(128)(2,1)S(1)}, bf16[3072]{0:T(1024)(128)(2,1)}, u32[]{:S(2)}) copy-start(bf16[3072]{0:T(1024)(128)(2,1)} %param.10) | copy-start | bytes 18436
  184.7 141.1 %reduce-scatter.7.cloned.1.call-start = ((), (), s32[]{:S(2)}) async-start(), calls=%async_computation.6 | async-start | bytes 1769472 | tf_op jit(solution)/shard_map/reduce_scatter | solution.py:36
Sparse Core Ops, SparseCore 0:
  57.6 38.7 reduce-scatter.4
  106.0 38.7 reduce-scatter.8
  148.4 19.6 all-gather.6
  169.5 19.6 all-gather.4
  192.5 65.6 reduce-scatter.10
  261.5 64.3 reduce-scatter.6
where the time goes:
time: 335 us; the launch traced here: 334 us
  waiting for transfers between devices  183 us (55%)
  blocking collectives  66 us (20%)
  matrix products  64.9 us (19%)
  between operations  13.5 us (4%)
  other arithmetic  4.79 us (1%)
    reduce_scatter x2, waiting for transfers between devices, local(): lax.psum_scatter(jnp.dot(hidden, down_weight, preferred_element_type=jnp....  121 us
    all_gather x2, blocking collectives, local(): lax.all_gather(local_rows, 'dp', axis=0, tiled=True)  66 us
    reduce_scatter x2, waiting for transfers between devices, local(): lax.psum_scatter(partial_up, 'tensor', scatter_dimension=0, tiled=True)  38.1 us
    dot_general x2, matrix products, local(): jnp.dot(hidden, down_weight, preferred_element_type=jnp.float32)  32.6 us
    dot_general x2, matrix products, local(): jnp.dot(lax.all_gather(local_rows, 'dp', axis=0, tiled=True), up_weight,...  32.3 us
    all_gather x2, waiting for transfers between devices, local(): hidden = lax.all_gather(hidden_share, 'tensor', axis=0, tiled=True)  23.4 us
  transfers between devices with their start and end apart: 6, of which 5 were waited for; matrix products, arithmetic and copies ran while one was open for 15% of the time, Pallas kernels for 0%

commit v1 on v0

--- a/solution.py
+++ b/solution.py
@@ -1,9 +1,15 @@
+import functools
+
 import jax
 import jax.numpy as jnp
 from jax import lax
+from jax.experimental import pallas as pl
+from jax.experimental.pallas import tpu as pltpu
 from jax.sharding import PartitionSpec as P
 
 RBLK = 128
+TILE = 512
+MESH = pl.DeviceIdType.MESH
 
 
 def activate(summed, up_bias, mask_table, first_row):
@@ -43,6 +49,264 @@
     return jnp.stack(results)
 
 
+def fused_kernel(nz, nt, tok, wu, wd, bias_u, mask, bias_d, out,
+                 x_all, w, pbuf, crecv, xsend, xrecv, hid, acc, ysend, yrecv, zsend, zrecv,
+                 tsem, wsem, ag_send, ag_recv, c_send, c_recv, x_send, x_recv, h_send, h_recv,
+                 y_send, y_recv, z_send, z_recv):
+    f32, bf16 = jnp.float32, jnp.bfloat16
+    steps, share, depth = tok.shape
+    rows = x_all.shape[1]
+    half = rows // 2
+    dp, t = lax.axis_index("dp"), lax.axis_index("tensor")
+    z, y = dp // 2, dp % 2
+    x, c = t // 2, t % 2
+    y_peer = (z * 2 + 1 - y, t)
+    x_peer = (dp, (1 - x) * 2 + c)
+    c_peer = (dp, x * 2 + 1 - c)
+    z_of = lambda k: lax.rem(z + k, nz)
+    own = pl.ds(pl.multiple_of(c * half, half), half)
+    other = pl.ds(pl.multiple_of((1 - c) * half, half), half)
+    block = lambda d: pl.ds(pl.multiple_of(d * share, share), share)
+
+    def rcopy(src, dst, ss, rs, dev):
+        return pltpu.make_async_remote_copy(
+            src_ref=src, dst_ref=dst, send_sem=ss, recv_sem=rs, device_id=dev, device_id_type=MESH
+        )
+
+    def up_load(j):
+        cols = pl.ds(pl.multiple_of(j * TILE, TILE), TILE)
+        return pltpu.make_async_copy(wu.at[:, cols], w.at[j], wsem.at[j])
+
+    def down_load(j):
+        lines = pl.ds(pl.multiple_of(j * TILE, TILE), TILE)
+        for n in range(depth // TILE):
+            part = pl.ds(n * TILE, TILE)
+            pltpu.make_async_copy(wd.at[lines, part], w.at[j, part], wsem.at[j]).start()
+
+    mine = [pltpu.make_async_copy(tok.at[s], x_all.at[s, block(dp)], tsem.at[s]) for s in range(steps)]
+    for copy in mine:
+        copy.start()
+
+    @pl.loop(0, nt)
+    def _(j):
+        up_load(j).start()
+
+    barrier = pltpu.get_barrier_semaphore()
+    peers = [y_peer, x_peer, c_peer] + [(z_of(k) * 2 + y, t) for k in range(1, nz)]
+    for peer in peers:
+        pl.semaphore_signal(barrier, inc=1, device_id=peer, device_id_type=MESH)
+    pl.semaphore_wait(barrier, len(peers))
+
+    def ag_copy(s, k, d, peer):
+        view = x_all.at[s, block(d)]
+        return rcopy(view, view, ag_send.at[s, k], ag_recv.at[s, d], peer)
+
+    def ag_sends(s):
+        mine[s].wait()
+        ag_copy(s, 0, dp, y_peer).start()
+        for k in range(1, nz):
+            ag_copy(s, k, dp, (z_of(k) * 2 + y, t)).start()
+
+    def ag_forward(s):
+        for k in range(1, nz):
+            d = z_of(k) * 2 + y
+            ag_copy(s, k, d, y_peer).wait_recv()
+            ag_copy(s, nz - 1 + k, d, y_peer).start()
+
+    def ag_finish(s):
+        for k in range(nz):
+            ag_copy(s, k, z_of(k) * 2 + 1 - y, y_peer).wait_recv()
+
+    def c_copy(q):
+        return rcopy(pbuf.at[q, other], crecv.at[q], c_send.at[q], c_recv.at[q], c_peer)
+
+    def x_copy(q):
+        return rcopy(xsend.at[q], xrecv.at[q], x_send.at[q], x_recv.at[q], x_peer)
+
+    def h_copy(q, lines):
+        return rcopy(hid.at[q, lines], hid.at[q, lines], h_send.at[q], h_recv.at[q], c_peer)
+
+    def up(s, j):
+        q = s * nt + j
+        pbuf[q] = jnp.dot(x_all[s], w[j], preferred_element_type=f32)
+        c_copy(q).start()
+
+    def mid(q):
+        c_copy(q).wait_recv()
+        total = pbuf[q, own] + crecv[q]
+        crecv[q] = total
+        xsend[q] = total.astype(bf16)
+        x_copy(q).start()
+
+    def act(s, j):
+        q = s * nt + j
+        x_copy(q).wait_recv()
+        pre = crecv[q] + xrecv[q].astype(f32) + bias_u[j]
+        hid[q, own] = (jnp.maximum(pre, 0.0) * mask[q]).astype(bf16)
+        h_copy(q, own).start()
+
+    def down(s, j):
+        q = s * nt + j
+        h_copy(q, other).wait_recv()
+        rows_in = hid[q]
+        for n in range(depth // TILE):
+            part = pl.ds(n * TILE, TILE)
+            acc[s, :, part] += jnp.dot(rows_in, w[j, part], preferred_element_type=f32)
+
+    def y_copy(s, k):
+        i = s * nz + k
+        return rcopy(ysend.at[i], yrecv.at[i], y_send.at[i], y_recv.at[i], y_peer)
+
+    def z_copy(s, k):
+        i = s * nz + k
+        return rcopy(zsend.at[i], zrecv.at[i], z_send.at[i], z_recv.at[i], (z_of(k) * 2 + y, t))
+
+    def rs_y(s):
+        for k in [*range(1, nz), 0]:
+            ysend[s * nz + k] = acc[s, block(z_of(k) * 2 + 1 - y)].astype(bf16)
+            y_copy(s, k).start()
+
+    def rs_z(s):
+        for k in range(1, nz):
+            y_copy(s, k).wait_recv()
+            pair = acc[s, block(z_of(k) * 2 + y)] + yrecv[s * nz + k].astype(f32)
+            zsend[s * nz + k] = pair.astype(bf16)
+            z_copy(s, k).start()
+
+    def rs_finish(s):
+        y_copy(s, 0).wait_recv()
+        total = acc[s, block(dp)] + yrecv[s * nz].astype(f32)
+        for k in range(1, nz):
+            z_copy(s, k).wait_recv()
+            total += zrecv[s * nz + k].astype(f32)
+        out[s] = (total + bias_d[...]).astype(bf16)
+
+    ag_sends(0)
+    ag_forward(0)
+    ag_sends(1)
+    acc[...] = jnp.zeros_like(acc)
+    ag_finish(0)
+    part_way = nt * 2 // 3
+
+    def first_step(j):
+        up_load(j).wait()
+        up(0, j)
+
+        @pl.when(j >= 1)
+        def _():
+            mid(j - 1)
+
+    pl.loop(0, part_way)(first_step)
+    ag_forward(1)
+    pl.loop(part_way, nt)(first_step)
+    mid(nt - 1)
+    ag_finish(1)
+
+    @pl.loop(0, nt)
+    def _(j):
+        up(1, j)
+
+        @pl.when(j >= 1)
+        def _():
+            mid(nt + j - 1)
+            down_load(j - 1)
+
+        act(0, j)
+
+    mid(2 * nt - 1)
+    down_load(nt - 1)
+
+    @pl.loop(0, nt)
+    def _(j):
+        up_load(j).wait()
+        down(0, j)
+
+    rs_y(0)
+    ahead = nt // 3
+
+    @pl.loop(0, ahead)
+    def _(j):
+        act(1, j)
+
+    rs_z(0)
+
+    @pl.loop(0, ahead - 1)
+    def _(j):
+        down(1, j)
+
+    @pl.loop(ahead, nt)
+    def _(j):
+        act(1, j)
+        down(1, j - 1)
+
+    down(1, nt - 1)
+    rs_y(1)
+    rs_finish(0)
+    rs_z(1)
+    rs_finish(1)
+
+    for s in range(steps):
+        for k in range(2 * nz - 1):
+            ag_copy(s, k, dp, y_peer).wait_send()
+        for k in range(nz):
+            y_copy(s, k).wait_send()
+        for k in range(1, nz):
+            z_copy(s, k).wait_send()
+
+    @pl.loop(0, steps * nt)
+    def _(q):
+        c_copy(q).wait_send()
+        x_copy(q).wait_send()
+        h_copy(q, own).wait_send()
+
+
+def fused(groups, tokens, up_weight, up_bias, down_weight, down_bias, active):
+    steps, share, depth = tokens.shape
+    hidden = up_weight.shape[1]
+    rows, nz, nt = groups * share, groups // 2, hidden // TILE
+    f32, bf16 = jnp.float32, jnp.bfloat16
+    width = hidden // active.shape[2]
+    mask = jnp.repeat(active.astype(f32).reshape(steps, -1), width, axis=1).reshape(steps * nt, 1, TILE)
+    any_space, vmem = pl.BlockSpec(memory_space=pl.ANY), pl.BlockSpec(memory_space=pltpu.VMEM)
+    dma = pltpu.SemaphoreType.DMA
+    half = rows // 2
+    return pl.pallas_call(
+        functools.partial(fused_kernel, nz, nt),
+        out_shape=jax.ShapeDtypeStruct(tokens.shape, bf16),
+        in_specs=[any_space, any_space, any_space, vmem, vmem, vmem],
+        out_specs=vmem,
+        scratch_shapes=[
+            pltpu.VMEM((steps, rows, depth), bf16),
+            pltpu.VMEM((nt, depth, TILE), bf16),
+            pltpu.VMEM((steps * nt, rows, TILE), f32),
+            pltpu.VMEM((steps * nt, half, TILE), f32),
+            pltpu.VMEM((steps * nt, half, TILE), bf16),
+            pltpu.VMEM((steps * nt, half, TILE), bf16),
+            pltpu.VMEM((steps * nt, rows, TILE), bf16),
+            pltpu.VMEM((steps, rows, depth), f32),
+        ]
+        + [pltpu.VMEM((steps * nz, share, depth), bf16)] * 4
+        + [
+            dma((steps,)),
+            dma((nt,)),
+            dma((steps, 2 * nz - 1)),
+            dma((steps, 2 * nz)),
+        ]
+        + [dma((steps * nt,))] * 6
+        + [dma((steps * nz,))] * 4,
+        compiler_params=pltpu.CompilerParams(
+            collective_id=0, has_side_effects=True, vmem_limit_bytes=67043328
+        ),
+    )(
+        tokens,
+        up_weight,
+        down_weight,
+        up_bias.astype(f32).reshape(nt, 1, TILE),
+        mask,
+        down_bias.astype(f32).reshape(1, depth),
+    )
+
+
 def solution(mesh):
     placed = (
         P(None, "dp", "tensor"),
@@ -52,6 +316,20 @@
         P("tensor"),
         P(None, None, "dp"),
     )
+    groups, columns = mesh.shape["dp"], mesh.shape["tensor"]
+
+    def body(*args):
+        steps, share, depth = args[0].shape
+        hidden, table = args[1].shape[1], args[5].shape
+        if (
+            (groups, columns, steps, table[1]) == (8, 4, 2, 1)
+            and share % 16 == 0
+            and depth % TILE == 0
+            and hidden % TILE == 0
+        ):
+            return fused(groups, *args)
+        return local(*args)
+
     return jax.shard_map(
-        local, mesh=mesh, in_specs=placed, out_specs=P(None, "dp", "tensor"), check_vma=False
+        body, mesh=mesh, in_specs=placed, out_specs=P(None, "dp", "tensor"), check_vma=False
     )

time: 335 us -> 95.5 us (0.29)
  waiting for transfers between devices: 183 us -> 0 us
  Pallas kernels: 0 us -> 89.5 us
  blocking collectives: 66 us -> 0 us
  matrix products: 64.9 us -> 0 us
  between operations: 13.5 us -> 0.01 us
    reduce_scatter x4 -> x0, waiting for transfers between devices: 159 us -> none  [the longest x2 121 us: local(): lax.psum_scatter(jnp.dot(hidden, down_weight, preferred_element_type=jnp....]
    pallas_call x0 -> x1, Pallas kernels: none -> 89.5 us  [fused(): pl.pallas_call(functools.partial(fused_kernel, nz, nt), out_shape=jax.Sha...]
    all_gather x2 -> x0, blocking collectives: 66 us -> none  [local(): lax.all_gather(local_rows, 'dp', axis=0, tiled=True)]
    dot_general x4 -> x0, matrix products: 64.9 us -> none  [the longest x2 32.6 us: local(): jnp.dot(hidden, down_weight, preferred_element_type=jnp.float32)]
    all_gather x2 -> x0, waiting for transfers between devices: 23.4 us -> none  [local(): hidden = lax.all_gather(hidden_share, 'tensor', axis=0, tiled=True)]
  transfers between devices with their start and end apart: 6 -> 0, of which waited for: 5 -> 0; matrix products, arithmetic and copies ran while one was open for 15% -> 0% of each run, Pallas kernels for 0% -> 0%
where the time goes in v1:
time: 95.5 us; the launch traced here: 95.1 us
  Pallas kernels  89.5 us (94%)
  other arithmetic  3.28 us (3%)
  local copies, waits for them, and re-layouts  2.31 us (2%)
    pallas_call x1, Pallas kernels, fused(): pl.pallas_call(functools.partial(fused_kernel, nz, nt), out_shape=jax.Sha...  89.5 us

profile of v1, /device:TPU:0, one launch (start us, length us, event | category | flops | bytes accessed | tf_op | source)
XLA Modules:
  0.0 95.1 jit_solution(6631237991106840489)
XLA Ops:
  0.0 0.7 convert_element_type.2
  0.7 1.3 %reshape.20 = f32[3072]{0:T(1024)} convert(bf16[3072]{0:T(1024)(128)(2,1)} %param.10) | non-fusion elementwise | flops 3072 | bytes 18432 | tf_op jit(solution)/shard_map/reshape | solution.py:306
  2.0 1.3 %reshape.18 = f32[6144]{0:T(1024)} convert(bf16[6144]{0:T(1024)(128)(2,1)} %param.8) | non-fusion elementwise | flops 6144 | bytes 36864 | tf_op jit(solution)/shard_map/reshape | solution.py:304
  3.3 0.7 broadcast_in_dim.3
  4.0 89.5 %shard_map.64 = bf16[2,16,3072]{2,1,0:T(8,128)(2,1)} custom-call(bf16[2,16,3072]{2,1,0:T(8,128)(2,1)} %tok.1, bf16[3072,6144]{1,0:T(8,128)(2,1)} %wu.1, bf16[6144,3072]{1,0:T(8,128)(2,1)} %wd.1, f32[12,1,512]{2,1,0:T(1,128)} %bitcast.5, f32[24,1,512]{2,1,0:T(1,128)} %bitcast.4, f32[1,3072]{1,0:T(1,128)} %bitcast.6), custom_call_target="tpu_custom_call" | custom-call | tf_op jit(solution)/shard_map/pallas_call | solution.py:273
  93.5 1.6 %copy.8 = bf16[2,16,3072]{2,1,0:T(8,128)(2,1)} copy(bf16[2,16,3072]{2,1,0:T(8,128)(2,1)} %shard_map.64) | data formatting | bytes 393216

commit v2 on v1

v2 whole, which is shorter than its diff:
```python
import functools

import jax
import jax.numpy as jnp
from jax import lax
from jax.experimental import pallas as pl
from jax.experimental.pallas import tpu as pltpu
from jax.sharding import PartitionSpec as P

RBLK = 128
TILE = 512
LAG = 3
MESH = pl.DeviceIdType.MESH


def activate(summed, up_bias, mask_table, first_row):
    row_count = summed.shape[0]
    blocks = mask_table.shape[1]
    row_ids = first_row + jnp.arange(row_count, dtype=jnp.int32)
    onehot = (
        row_ids[:, None] // RBLK == jnp.arange(mask_table.shape[0], dtype=jnp.int32)[None, :]
    ).astype(jnp.float32)
    row_mask = jnp.dot(onehot, mask_table.astype(jnp.float32))
    preact = jnp.maximum(summed + up_bias.astype(jnp.float32), 0.0)
    gated_rows = preact.reshape(row_count, blocks, -1) * row_mask[:, :, None]
    return gated_rows.reshape(row_count, -1).astype(jnp.bfloat16)


def local(tokens, up_weight, up_bias, down_weight, down_bias, active):
    results = []
    for step_index in range(tokens.shape[0]):
        local_rows = tokens[step_index]
        mask_table = active[step_index]
        partial_up = jnp.dot(
            lax.all_gather(local_rows, "dp", axis=0, tiled=True),
            up_weight,
            preferred_element_type=jnp.float32,
        )
        row_share = lax.psum_scatter(partial_up, "tensor", scatter_dimension=0, tiled=True)
        first_row = lax.axis_index("tensor") * row_share.shape[0]
        hidden_share = activate(row_share, up_bias, mask_table, first_row)
        hidden = lax.all_gather(hidden_share, "tensor", axis=0, tiled=True)
        mixed_rows = lax.psum_scatter(
            jnp.dot(hidden, down_weight, preferred_element_type=jnp.float32),
            "dp",
            scatter_dimension=0,
            tiled=True,
        )
        results.append((mixed_rows + down_bias.astype(jnp.float32)).astype(jnp.bfloat16))
    return jnp.stack(results)


def fused_kernel(nz, nt, tok, wu, wd, bias_u, active, out,
                 x_all, w, pbuf, crecv, xsend, xrecv, hid, acc, ysend, yrecv, zsend, zrecv,
                 tsem, wsem, ag_send, ag_recv, c_send, c_recv, x_send, x_recv, h_send, h_recv,
                 y_send, y_recv, z_send, z_recv):
    f32, bf16 = jnp.float32, jnp.bfloat16
    steps, share, depth = tok.shape
    rows = x_all.shape[1]
    half = rows // 2
    dp, t = lax.axis_index("dp"), lax.axis_index("tensor")
    z, y = dp // 2, dp % 2
    x, c = t // 2, t % 2
    y_peer = (z * 2 + 1 - y, t)
    x_peer = (dp, (1 - x) * 2 + c)
    c_peer = (dp, x * 2 + 1 - c)
    z_of = lambda k: lax.rem(z + k, nz)
    own = pl.ds(pl.multiple_of(c * half, half), half)
    other = pl.ds(pl.multiple_of((1 - c) * half, half), half)
    cols = lambda j: pl.ds(pl.multiple_of(j * TILE, TILE), TILE)
    nc = depth // TILE
    spans = nt // nc
    block = lambda d: pl.ds(pl.multiple_of(d * share, share), share)

    def rcopy(src, dst, ss, rs, dev):
        return pltpu.make_async_remote_copy(
            src_ref=src, dst_ref=dst, send_sem=ss, recv_sem=rs, device_id=dev, device_id_type=MESH
        )

    def up_load(j):
        return pltpu.make_async_copy(wu.at[:, cols(j)], w.at[j], wsem.at[j])

    def down_load(i):
        n, part = i // spans, i % spans
        lines = pl.ds(pl.multiple_of(part * depth, depth), depth)
        return pltpu.make_async_copy(wd.at[lines, cols(n)], w.at[i], wsem.at[i])

    mine = [pltpu.make_async_copy(tok.at[s], x_all.at[s, block(dp)], tsem.at[s]) for s in range(steps)]
    for copy in mine:
        copy.start()

    @pl.loop(0, nt)
    def _(j):
        up_load(j).start()

    barrier = pltpu.get_barrier_semaphore()
    peers = [y_peer, x_peer, c_peer] + [(z_of(k) * 2 + y, t) for k in range(1, nz)]
    for peer in peers:
        pl.semaphore_signal(barrier, inc=1, device_id=peer, device_id_type=MESH)
    pl.semaphore_wait(barrier, len(peers))

    def ag_copy(s, k, d, peer):
        view = x_all.at[s, block(d)]
        return rcopy(view, view, ag_send.at[s, k], ag_recv.at[s, d], peer)

    def ag_sends(s):
        mine[s].wait()
        ag_copy(s, 0, dp, y_peer).start()
        for k in range(1, nz):
            ag_copy(s, k, dp, (z_of(k) * 2 + y, t)).start()

    def ag_forward(s, k):
        d = z_of(k) * 2 + y
        ag_copy(s, k, d, y_peer).wait_recv()
        ag_copy(s, nz - 1 + k, d, y_peer).start()

    def ag_finish(s):
        for k in range(nz):
            ag_copy(s, k, z_of(k) * 2 + 1 - y, y_peer).wait_recv()

    def c_copy(q):
        return rcopy(pbuf.at[q, other], crecv.at[q], c_send.at[q], c_recv.at[q], c_peer)

    def x_copy(q):
        return rcopy(xsend.at[q], xrecv.at[q], x_send.at[q], x_recv.at[q], x_peer)

    def h_copy(s, j, lines):
        view, q = hid.at[s, lines, cols(j)], s * nt + j
        return rcopy(view, view, h_send.at[q], h_recv.at[q], c_peer)

    def up(s, j):
        q = s * nt + j
        pbuf[q] = jnp.dot(x_all[s], w[j], preferred_element_type=f32)
        c_copy(q).start()

    def mid(q):
        c_copy(q).wait_recv()
        total = pbuf[q, own] + crecv[q]
        crecv[q] = total
        xsend[q] = total.astype(bf16)
        x_copy(q).start()

    def act(s, j):
        q = s * nt + j
        x_copy(q).wait_recv()
        bias = bias_u[cols(j)].astype(f32).reshape(1, TILE)
        pre = jnp.maximum(crecv[q] + xrecv[q].astype(f32) + bias, 0.0)
        blocks = active.shape[2] // nt
        width = TILE // blocks
        for b in range(blocks):
            gate = active[s, 0, j * blocks + b].astype(f32)
            lanes = pl.ds(pl.multiple_of(j * TILE + b * width, width), width)
            hid[s, own, lanes] = (pre[:, b * width : (b + 1) * width] * gate).astype(bf16)
        h_copy(s, j, own).start()

    def hidden_ready(s):
        @pl.loop(0, nt)
        def _(j):
            h_copy(s, j, other).wait_recv()

    def y_copy(i):
        return rcopy(ysend.at[i], yrecv.at[i], y_send.at[i], y_recv.at[i], y_peer)

    def z_copy(i, k):
        q = i * nz + k
        return rcopy(zsend.at[q], zrecv.at[q], z_send.at[q], z_recv.at[q], (z_of(k) * 2 + y, t))

    def down(s, n):
        total = jnp.zeros((rows, TILE), f32)
        for part in range(spans):
            total += jnp.dot(
                hid[s, :, part * depth : (part + 1) * depth], w[n * spans + part], preferred_element_type=f32
            )
        acc[s, :, cols(n)] = total
        i = s * nc + n
        for zz in range(nz):
            ysend[i, zz] = acc[s, block(zz * 2 + 1 - y), cols(n)].astype(bf16)
        y_copy(i).start()

    def rs_z(s, n):
        i = s * nc + n
        y_copy(i).wait_recv()
        for k in range(1, nz):
            pair = acc[s, block(z_of(k) * 2 + y), cols(n)] + yrecv[i, z_of(k)].astype(f32)
            zsend[i * nz + k] = pair.astype(bf16)
            z_copy(i, k).start()

    def rs_finish(s, n):
        i = s * nc + n
        total = acc[s, block(dp), cols(n)] + yrecv[i, z].astype(f32)
        for k in range(1, nz):
            z_copy(i, k).wait_recv()
            total += zrecv[i * nz + k].astype(f32)
        out[s, :, cols(n)] = total

    ag_sends(0)
    for k in range(1, nz):
        ag_forward(0, k)
    ag_sends(1)
    ag_finish(0)

    def first_step(j):
        up_load(j).wait()
        up(0, j)

        @pl.when(j >= 1)
        def _():
            mid(j - 1)

    cut = [nt * k // (nz + 1) for k in range(nz)] + [nt]
    for k in range(nz):
        pl.loop(cut[k], cut[k + 1])(first_step)
        if k + 1 < nz:
            ag_forward(1, k + 1)
    mid(nt - 1)
    ag_finish(1)

    @pl.loop(0, nt)
    def _(j):
        up(1, j)

        @pl.when(j >= 1)
        def _():
            mid(nt + j - 1)
            down_load(j - 1).start()

        act(0, j)

    mid(2 * nt - 1)
    down_load(nt - 1).start()
    hidden_ready(0)

    @pl.loop(0, nc)
    def _(n):
        for part in range(spans):
            down_load(n * spans + part).wait()
        down(0, n)

        @pl.when(n >= LAG)
        def _():
            rs_z(0, n - LAG)

    @pl.loop(0, nt // 2)
    def _(j):
        act(1, j)

    @pl.loop(nc - LAG, nc)
    def _(n):
        rs_z(0, n)

    @pl.loop(nt // 2, nt)
    def _(j):
        act(1, j)

    hidden_ready(1)

    @pl.loop(0, nc)
    def _(n):
        down(1, n)

        @pl.when(n >= LAG)
        def _():
            rs_z(1, n - LAG)

    @pl.loop(nc - LAG, nc)
    def _(n):
        rs_z(1, n)

    for s in range(steps):
        @pl.loop(0, nc)
        def _(n):
            rs_finish(s, n)

    for s in range(steps):
        for k in range(2 * nz - 1):
            ag_copy(s, k, dp, y_peer).wait_send()

    @pl.loop(0, steps * nc)
    def _(i):
        y_copy(i).wait_send()
        for k in range(1, nz):
            z_copy(i, k).wait_send()

    for s in range(steps):
        @pl.loop(0, nt)
        def _(j):
            c_copy(s * nt + j).wait_send()
            x_copy(s * nt + j).wait_send()
            h_copy(s, j, own).wait_send()


def fused(groups, tokens, up_weight, up_bias, down_weight, down_bias, active):
    steps, share, depth = tokens.shape
    hidden = up_weight.shape[1]
    rows, nz, nt, nc = groups * share, groups // 2, hidden // TILE, depth // TILE
    f32, bf16 = jnp.float32, jnp.bfloat16
    any_space, vmem = pl.BlockSpec(memory_space=pl.ANY), pl.BlockSpec(memory_space=pltpu.VMEM)
    smem = pl.BlockSpec(memory_space=pltpu.SMEM)
    dma = pltpu.SemaphoreType.DMA
    half = rows // 2
    mixed = pl.pallas_call(
        functools.partial(fused_kernel, nz, nt),
        out_shape=jax.ShapeDtypeStruct(tokens.shape, f32),
        in_specs=[any_space, any_space, any_space, vmem, smem],
        out_specs=vmem,
        scratch_shapes=[
            pltpu.VMEM((steps, rows, depth), bf16),
            pltpu.VMEM((nt, depth, TILE), bf16),
            pltpu.VMEM((steps * nt, rows, TILE), f32),
            pltpu.VMEM((steps * nt, half, TILE), f32),
            pltpu.VMEM((steps * nt, half, TILE), bf16),
            pltpu.VMEM((steps * nt, half, TILE), bf16),
            pltpu.VMEM((steps, rows, hidden), bf16),
            pltpu.VMEM((steps, rows, depth), f32),
        ]
        + [pltpu.VMEM((steps * nc, nz, share, TILE), bf16)] * 2
        + [pltpu.VMEM((steps * nc * nz, share, TILE), bf16)] * 2
        + [
            dma((steps,)),
            dma((nt,)),
            dma((steps, 2 * nz - 1)),
            dma((steps, 2 * nz)),
        ]
        + [dma((steps * nt,))] * 6
        + [dma((steps * nc,))] * 2
        + [dma((steps * nc * nz,))] * 2,
        compiler_params=pltpu.CompilerParams(
            collective_id=0, has_side_effects=True, vmem_limit_bytes=67043328
        ),
    )(tokens, up_weight, down_weight, up_bias, active)
    return (mixed + down_bias.astype(f32)).astype(bf16)


def solution(mesh):
    placed = (
        P(None, "dp", "tensor"),
        P("tensor", "dp"),
        P("dp"),
        P("dp", "tensor"),
        P("tensor"),
        P(None, None, "dp"),
    )
    groups, columns = mesh.shape["dp"], mesh.shape["tensor"]

    def body(*args):
        steps, share, depth = args[0].shape
        hidden, table = args[1].shape[1], args[5].shape
        if (
            (groups, columns, steps, table[1]) == (8, 4, 2, 1)
            and share % 16 == 0
            and depth % TILE == 0
            and hidden % depth == 0
            and (hidden // TILE) and table[2] % (hidden // TILE) == 0
            and depth // TILE > LAG
        ):
            return fused(groups, *args)
        return local(*args)

    return jax.shard_map(
        body, mesh=mesh, in_specs=placed, out_specs=P(None, "dp", "tensor"), check_vma=False
    )
```

time: 95.5 us -> 84.2 us (0.88)
  Pallas kernels: 89.5 us -> 80.9 us
  local copies, waits for them, and re-layouts: 2.31 us -> 0 us
    pallas_call x1, Pallas kernels: 89.5 us -> 80.9 us  [fused(): pl.pallas_call(functools.partial(fused_kernel, nz, nt), out_shape=jax.Sha...]
    reshape x2 -> x0, other arithmetic: 2.6 us -> none  [the longest x1 1.31 us: fused(): up_bias.astype(f32).reshape(nt, 1, TILE)]
    convert_element_type x1 -> x2, other arithmetic: 0.68 us -> 2.99 us  [fused(): return (mixed + down_bias.astype(f32)).astype(bf16)]
    unnamed x1 -> x0, local copies, waits for them, and re-layouts: 1.62 us -> none
where the time goes in v2:
time: 84.2 us; the launch traced here: 83.9 us
  Pallas kernels  80.9 us (96%)
  other arithmetic  2.99 us (4%)
    pallas_call x1, Pallas kernels, fused(): pl.pallas_call(functools.partial(fused_kernel, nz, nt), out_shape=jax.Sha...  80.9 us
    convert_element_type x2, other arithmetic, fused(): return (mixed + down_bias.astype(f32)).astype(bf16)  2.99 us

profile of v2, /device:TPU:0, one launch (start us, length us, event | category | flops | bytes accessed | tf_op | source)
XLA Modules:
  0.0 83.9 jit_solution(16933659365572903243)
XLA Ops:
  0.0 1.3 %convert_element_type.6 = f32[3072]{0:T(1024)} convert(bf16[3072]{0:T(1024)(128)(2,1)} %param.10) | non-fusion elementwise | flops 3072 | bytes 18432 | tf_op jit(solution)/shard_map/convert_element_type | solution.py:331
  1.3 80.9 %shard_map.64 = f32[2,16,3072]{2,1,0:T(8,128)} custom-call(bf16[2,16,3072]{2,1,0:T(8,128)(2,1)} %tok.1, bf16[3072,6144]{1,0:T(8,128)(2,1)} %wu.1, bf16[6144,3072]{1,0:T(8,128)(2,1)} %wd.1, bf16[6144]{0:T(1024)(128)(2,1)} %bias_u.1, s32[2,1,48]{2,1,0:T(1,128)} %active.1), custom_call_target="tpu_custom_call" | custom-call | tf_op jit(solution)/shard_map/pallas_call | solution.py:301
  82.2 1.7 %add_convert_fusion = bf16[2,16,3072]{2,1,0:T(8,128)(2,1)} fusion(f32[2,16,3072]{2,1,0:T(8,128)} %shard_map.64, f32[3072]{0:T(1024)} %convert_element_type.6), kind=kLoop, calls=%fused_computation | loop fusion | flops 196608 | bytes 602112 | tf_op jit(solution)/shard_map/convert_element_type | solution.py:331

commit v3 on v2

--- a/solution.py
+++ b/solution.py
@@ -252,12 +252,20 @@
     def _(j):
         act(1, j)
 
+    @pl.loop(0, nc - LAG)
+    def _(n):
+        rs_finish(0, n)
+
     hidden_ready(1)
 
     @pl.loop(0, nc)
     def _(n):
         down(1, n)
 
+        @pl.when(n < LAG)
+        def _():
+            rs_finish(0, nc - LAG + n)
+
         @pl.when(n >= LAG)
         def _():
             rs_z(1, n - LAG)
@@ -266,10 +274,9 @@
     def _(n):
         rs_z(1, n)
 
-    for s in range(steps):
-        @pl.loop(0, nc)
-        def _(n):
-            rs_finish(s, n)
+    @pl.loop(0, nc)
+    def _(n):
+        rs_finish(1, n)
 
     for s in range(steps):
         for k in range(2 * nz - 1):

time: 84.2 us -> 84.2 us (level)
  no operation moved by 1% of the time
where the time goes in v3:
time: 84.2 us; the launch traced here: 83.9 us
  Pallas kernels  80.9 us (96%)
  other arithmetic  2.99 us (4%)
    pallas_call x1, Pallas kernels, fused(): pl.pallas_call(functools.partial(fused_kernel, nz, nt), out_shape=jax.Sha...  80.9 us
    convert_element_type x2, other arithmetic, fused(): return (mixed + down_bias.astype(f32)).astype(bf16)  2.99 us

profile of v3, /device:TPU:0, one launch (start us, length us, event | category | flops | bytes accessed | tf_op | source)
XLA Modules:
  0.0 83.9 jit_solution(15068947724915697190)
XLA Ops:
  0.0 1.3 %convert_element_type.6 = f32[3072]{0:T(1024)} convert(bf16[3072]{0:T(1024)(128)(2,1)} %param.10) | non-fusion elementwise | flops 3072 | bytes 18432 | tf_op jit(solution)/shard_map/convert_element_type | solution.py:338
  1.3 80.9 %shard_map.64 = f32[2,16,3072]{2,1,0:T(8,128)} custom-call(bf16[2,16,3072]{2,1,0:T(8,128)(2,1)} %tok.1, bf16[3072,6144]{1,0:T(8,128)(2,1)} %wu.1, bf16[6144,3072]{1,0:T(8,128)(2,1)} %wd.1, bf16[6144]{0:T(1024)(128)(2,1)} %bias_u.1, s32[2,1,48]{2,1,0:T(1,128)} %active.1), custom_call_target="tpu_custom_call" | custom-call | tf_op jit(solution)/shard_map/pallas_call | solution.py:308
  82.2 1.7 %add_convert_fusion = bf16[2,16,3072]{2,1,0:T(8,128)(2,1)} fusion(f32[2,16,3072]{2,1,0:T(8,128)} %shard_map.64, f32[3072]{0:T(1024)} %convert_element_type.6), kind=kLoop, calls=%fused_computation | loop fusion | flops 196608 | bytes 602112 | tf_op jit(solution)/shard_map/convert_element_type | solution.py:338
